TPU v7x, 32 devices: a whole 2x2x4 slice. The times are simulated.
32 devices in a mesh: dp: 8 (over y, x, core), mp: 4 (over z).
Axes of the slice: x: 2, y: 2, z: 4, core: 2. Of those that a mesh axis runs over, the one named last changes fastest.
Arguments:
- tokens: bfloat16 [16, 512, 1024], P('dp', 'mp'), may hold values from -6 to 6
- memory: bfloat16 [16, 512, 1024], P('dp', 'mp'), may hold values from -6 to 6
- compressed: bfloat16 [16, 512, 1024], P('dp', 'mp'), may hold values from -6 to 6
- valid_counts: int32 [16], P('dp'), may hold values from 64 to 512, as said below
- attention_norm_gain: float32 [1024], replicated, may hold values from 0.5 to 1.5
- attention_norm_bias: float32 [1024], replicated, may hold values from -1.75 to 1.75
- query_projection: bfloat16 [1024, 1024], P(None, 'mp'), may hold values from -0.1875 to 0.1875
- key_projection: bfloat16 [1024, 1024], P(None, 'mp'), may hold values from -0.1875 to 0.1875
- value_projection: bfloat16 [1024, 1024], P(None, 'mp'), may hold values from -0.1875 to 0.1875
- out_weight: bfloat16 [1024, 1024], P('mp'), may hold values from -2 to 2
- feedforward_norm_gain: float32 [1024], replicated, may hold values from 0.5 to 1.5
- feedforward_norm_bias: float32 [1024], replicated, may hold values from -1.75 to 1.75
- up_weight: bfloat16 [1024, 4096], P(None, 'mp'), may hold values from -0.1875 to 0.1875
- up_bias: float32 [4096], P('mp'), may hold values from -3 to 3
- down_weight: bfloat16 [4096, 1024], P('mp'), may hold values from -0.09375 to 0.09375
- down_bias: float32 [1024], replicated, may hold values from -3 to 3
- squeeze_weight: bfloat16 [3072, 1024], replicated, may hold values from -0.109375 to 0.109375
- cotangent: bfloat16 [16, 512, 1024], P('dp', 'mp'), may hold values from -6 to 6
Outputs:
- output: bfloat16 [16, 512, 1024], P('dp', 'mp')
- tokens_grad: float32 [16, 512, 1024], P('dp', 'mp')
- attention_gain_gradient: float32 [1024], replicated
- first_bias_grad: float32 [1024], replicated
- query_weight_grad: float32 [1024, 1024], P(None, 'mp')
- key_weight_grad: float32 [1024, 1024], P(None, 'mp')
- value_weight_grad: float32 [1024, 1024], P(None, 'mp')
- out_weight_grad: float32 [1024, 1024], P('mp')
- feedforward_gain_gradient: float32 [1024], replicated
- second_bias_grad: float32 [1024], replicated
- up_weight_grad: float32 [1024, 4096], P(None, 'mp')
- up_bias_grad: float32 [4096], P('mp')
- down_weight_grad: float32 [4096, 1024], P('mp')
- down_bias_grad: float32 [1024], replicated
- new_memory: bfloat16 [16, 512, 1024], P('dp', 'mp')
- new_compressed: bfloat16 [16, 512, 1024], P('dp', 'mp')
Inputs may be any that keep to these rules, and one draw needn't show every extreme that they name: The first valid_counts tokens of a segment are real, the rest padding.
All inputs are finite; a program needn't handle non-finite values.
Results may differ from a plain program's by a relative error of at most 0.015.
Values may be sent and summed in bfloat16 or wider, within the bound.
A program may use at most 192 MiB of HBM per device.

v0:
```python
import jax
import jax.numpy as jnp
from jax import lax
from jax.sharding import PartitionSpec as P

HEAD_DIM = 128
RATE = 3


def apply_layer_norm(rows):
    center = jnp.mean(rows, axis=-1, keepdims=True)
    centered = rows - center
    spread = jnp.mean(centered * centered, axis=-1, keepdims=True)
    inverse_deviation = lax.rsqrt(spread + 1e-05)
    return (centered * inverse_deviation, inverse_deviation)


def norm_backward_pass(input_gradient, standardized_rows, inverse_deviation, scale_factor):
    scaled_rows = input_gradient * scale_factor
    attention_norm_mean = jnp.mean(scaled_rows, axis=-1, keepdims=True)
    feedforward_norm_mean = jnp.mean(scaled_rows * standardized_rows, axis=-1, keepdims=True)
    return inverse_deviation * (
        scaled_rows - attention_norm_mean - standardized_rows * feedforward_norm_mean
    )


def squeeze_rows(old_comp, old_mem, fresh, valid_count, offset, own_rows, squeeze_weight):
    features = old_mem.shape[1]
    joined = jnp.concatenate([old_mem, fresh], axis=0)
    new_memory = lax.dynamic_slice_in_dim(joined, valid_count + offset, own_rows, 0)
    comp_len = old_comp.shape[0]
    evicted = valid_count // RATE
    first_row = evicted + offset
    window_start = jnp.maximum(first_row - comp_len, 0)
    padded = jnp.concatenate(
        [old_mem, jnp.zeros((RATE * own_rows, features), jnp.bfloat16)], axis=0
    )
    window = lax.dynamic_slice_in_dim(padded, window_start * RATE, RATE * own_rows, 0)
    squeezed = jnp.dot(
        window.reshape(own_rows, RATE * features),
        squeeze_weight,
        preferred_element_type=jnp.float32,
    ).astype(jnp.bfloat16)
    positions = first_row + jnp.arange(own_rows)
    from_old = jnp.take(old_comp, jnp.clip(positions, 0, comp_len - 1), axis=0)
    from_new = jnp.take(
        squeezed, jnp.clip(positions - comp_len - window_start, 0, own_rows - 1), axis=0
    )
    new_compressed = jnp.where((positions < comp_len)[:, None], from_old, from_new)
    return (new_memory, new_compressed)


def per_device(
    tokens,
    memory,
    compressed,
    valid_counts,
    attention_norm_gain,
    attention_norm_bias,
    query_projection,
    key_projection,
    value_projection,
    out_weight,
    feedforward_norm_gain,
    feedforward_norm_bias,
    up_weight,
    up_bias,
    down_weight,
    down_bias,
    squeeze_weight,
    cotangent,
):
    batch_segs, own_rows, features = tokens.shape
    offset = lax.axis_index("mp") * own_rows
    old_comp, old_mem, fresh = (
        lax.all_gather(compressed, "mp", axis=1, tiled=True),
        lax.all_gather(memory, "mp", axis=1, tiled=True),
        lax.all_gather(tokens, "mp", axis=1, tiled=True),
    )
    seg_len = fresh.shape[1]
    prior_rows = old_comp.shape[1] + old_mem.shape[1]
    context_tokens = jnp.concatenate([old_comp, old_mem, fresh], axis=1).astype(jnp.float32)
    ctx_len = context_tokens.shape[1]
    standardized_full, inverse_deviation_full = apply_layer_norm(context_tokens)
    normed_rows = (standardized_full * attention_norm_gain + attention_norm_bias).astype(
        jnp.bfloat16
    )
    token_rows_normed = normed_rows[:, prior_rows:]
    queries = jnp.einsum(
        "xhp,pj->xhj", token_rows_normed, query_projection, preferred_element_type=jnp.float32
    ).astype(jnp.bfloat16)
    key_rows = jnp.einsum(
        "xhp,pj->xhj", normed_rows, key_projection, preferred_element_type=jnp.float32
    ).astype(jnp.bfloat16)
    values = jnp.einsum(
        "xhp,pj->xhj", normed_rows, value_projection, preferred_element_type=jnp.float32
    ).astype(jnp.bfloat16)
    local_heads = query_projection.shape[1] // HEAD_DIM
    score_scale = HEAD_DIM ** (-0.5)

    def by_heads(matrix):
        return matrix.reshape(matrix.shape[0], matrix.shape[1], local_heads, HEAD_DIM)

    query_pos = jnp.arange(seg_len)[:, None]
    key_pos = jnp.arange(ctx_len)[None, :] - prior_rows
    allowed = (key_pos[None] < 0) | (key_pos <= query_pos)[None] & (
        key_pos[None] < valid_counts[:, None, None]
    )

    def scores_of(query_in, key_in):
        raw = (
            jnp.einsum(
                "gqhe,gkhe->ghqk",
                by_heads(query_in),
                by_heads(key_in),
                preferred_element_type=jnp.float32,
            )
            * score_scale
        )
        return jnp.where(allowed[:, None], raw, -1e30)

    scores = scores_of(queries, key_rows)
    peak_score = jnp.max(scores, axis=-1, keepdims=True)
    exponent = jnp.exp(scores - peak_score)
    exp_total = jnp.sum(exponent, axis=-1, keepdims=True)
    log_total = peak_score + jnp.log(exp_total)
    probs_low = (exponent / exp_total).astype(jnp.bfloat16)
    mixed_heads = jnp.einsum(
        "ghqk,gkhe->gqhe", probs_low, by_heads(values), preferred_element_type=jnp.float32
    ).astype(jnp.bfloat16)
    mixed_heads = mixed_heads.reshape(batch_segs, seg_len, local_heads * HEAD_DIM)
    partial_attn = jnp.einsum(
        "gsc,cd->gsd", mixed_heads, out_weight, preferred_element_type=jnp.float32
    )
    attention = lax.psum_scatter(partial_attn, "mp", scatter_dimension=1, tiled=True)
    residual_stream = tokens.astype(jnp.float32) + attention
    standardized_feedforward, inverse_deviation_feedforward = apply_layer_norm(residual_stream)
    feedforward_input = (
        standardized_feedforward * feedforward_norm_gain + feedforward_norm_bias
    ).astype(jnp.bfloat16)
    second_all = lax.all_gather(feedforward_input, "mp", axis=1, tiled=True)
    upper_in = (
        jnp.einsum("gsd,df->gsf", second_all, up_weight, preferred_element_type=jnp.float32)
        + up_bias
    )
    active, gelu_back = jax.vjp(jax.nn.gelu, upper_in)
    active_low = active.astype(jnp.bfloat16)
    partial_ffn = jnp.einsum(
        "gsf,fd->gsd", active_low, down_weight, preferred_element_type=jnp.float32
    )
    down_out = lax.psum_scatter(
        partial_ffn.astype(jnp.bfloat16), "mp", scatter_dimension=1, tiled=True
    ).astype(jnp.float32)
    output = (residual_stream + down_out + down_bias).astype(jnp.bfloat16)

    def update_one(comp_seg, mem_seg, fresh_seg, valid_count):
        return squeeze_rows(
            comp_seg, mem_seg, fresh_seg, valid_count, offset, own_rows, squeeze_weight
        )

    new_memory, new_compressed = jax.vmap(update_one)(old_comp, old_mem, fresh, valid_counts)
    output_gradient = cotangent.astype(jnp.float32)
    down_bias_grad = jnp.sum(output_gradient, axis=(0, 1))
    grad_all = lax.all_gather(cotangent, "mp", axis=1, tiled=True)
    down_weight_grad = jnp.einsum(
        "gsf,gsd->fd", active_low, grad_all, preferred_element_type=jnp.float32
    )
    grad_active = jnp.einsum(
        "gsd,fd->gsf", grad_all, down_weight, preferred_element_type=jnp.float32
    )
    grad_upper = gelu_back(grad_active)[0].astype(jnp.bfloat16)
    up_weight_grad = jnp.einsum(
        "gsd,gsf->df", second_all, grad_upper, preferred_element_type=jnp.float32
    )
    up_bias_grad = jnp.sum(grad_upper.astype(jnp.float32), axis=(0, 1))
    partial_second = jnp.einsum(
        "gsf,df->gsd", grad_upper, up_weight, preferred_element_type=jnp.float32
    )
    feedforward_gradient = lax.psum_scatter(partial_second, "mp", scatter_dimension=1, tiled=True)
    feedforward_gain_gradient = jnp.sum(
        feedforward_gradient * standardized_feedforward, axis=(0, 1)
    )
    second_bias_grad = jnp.sum(feedforward_gradient, axis=(0, 1))
    residual_gradient = output_gradient + norm_backward_pass(
        feedforward_gradient,
        standardized_feedforward,
        inverse_deviation_feedforward,
        feedforward_norm_gain,
    )
    grad_resid_all = lax.all_gather(
        residual_gradient.astype(jnp.bfloat16), "mp", axis=1, tiled=True
    )
    out_weight_grad = jnp.einsum(
        "gsc,gsd->cd", mixed_heads, grad_resid_all, preferred_element_type=jnp.float32
    )
    grad_mixed = jnp.einsum(
        "gsd,cd->gsc", grad_resid_all, out_weight, preferred_element_type=jnp.float32
    ).astype(jnp.bfloat16)
    probs_again = jnp.exp(scores_of(queries, key_rows) - log_total)
    grad_probs = jnp.einsum(
        "gqhe,gkhe->ghqk",
        by_heads(grad_mixed),
        by_heads(values),
        preferred_element_type=jnp.float32,
    )
    row_dot = jnp.sum(probs_again * grad_probs, axis=-1, keepdims=True)
    grad_scores = (probs_again * (grad_probs - row_dot)).astype(jnp.bfloat16)
    query_gradient = (
        score_scale
        * jnp.einsum(
            "ghqk,gkhe->gqhe", grad_scores, by_heads(key_rows), preferred_element_type=jnp.float32
        )
    ).astype(jnp.bfloat16)
    key_gradient = (
        score_scale
        * jnp.einsum(
            "ghqk,gqhe->gkhe", grad_scores, by_heads(queries), preferred_element_type=jnp.float32
        )
    ).astype(jnp.bfloat16)
    value_gradient = jnp.einsum(
        "ghqk,gqhe->gkhe",
        probs_again.astype(jnp.bfloat16),
        by_heads(grad_mixed),
        preferred_element_type=jnp.float32,
    ).astype(jnp.bfloat16)
    query_gradient = query_gradient.reshape(batch_segs, seg_len, -1)
    key_gradient = key_gradient.reshape(batch_segs, ctx_len, -1)
    value_gradient = value_gradient.reshape(batch_segs, ctx_len, -1)
    query_weight_grad = jnp.einsum(
        "nja,njr->ar", token_rows_normed, query_gradient, preferred_element_type=jnp.float32
    )
    key_weight_grad = jnp.einsum(
        "nja,njr->ar", normed_rows, key_gradient, preferred_element_type=jnp.float32
    )
    value_weight_grad = jnp.einsum(
        "nja,njr->ar", normed_rows, value_gradient, preferred_element_type=jnp.float32
    )
    partial_normed = jnp.einsum(
        "xmo,qo->xmq", key_gradient, key_projection, preferred_element_type=jnp.float32
    )
    partial_normed = partial_normed + jnp.einsum(
        "xmo,qo->xmq", value_gradient, value_projection, preferred_element_type=jnp.float32
    )
    partial_normed = partial_normed.at[:, prior_rows:].add(
        jnp.einsum(
            "xmo,qo->xmq", query_gradient, query_projection, preferred_element_type=jnp.float32
        )
    )
    partial_normed = partial_normed.reshape(batch_segs, 3, seg_len, features)
    normed_gradient = lax.psum_scatter(
        partial_normed.astype(jnp.bfloat16), "mp", scatter_dimension=2, tiled=True
    ).astype(jnp.float32)
    segment_context = jnp.stack([compressed, memory, tokens], axis=1).astype(jnp.float32)
    standardized_segment, inverse_deviation_segment = apply_layer_norm(segment_context)
    attention_gain_gradient = jnp.sum(normed_gradient * standardized_segment, axis=(0, 1, 2))
    first_bias_grad = jnp.sum(normed_gradient, axis=(0, 1, 2))
    tokens_grad = residual_gradient + norm_backward_pass(
        normed_gradient[:, 2],
        standardized_segment[:, 2],
        inverse_deviation_segment[:, 2],
        attention_norm_gain,
    )
    summed = (
        lax.psum(query_weight_grad.astype(jnp.bfloat16), "dp").astype(jnp.float32),
        lax.psum(key_weight_grad.astype(jnp.bfloat16), "dp").astype(jnp.float32),
        lax.psum(value_weight_grad.astype(jnp.bfloat16), "dp").astype(jnp.float32),
        lax.psum(out_weight_grad.astype(jnp.bfloat16), "dp").astype(jnp.float32),
        lax.psum(up_weight_grad.astype(jnp.bfloat16), "dp").astype(jnp.float32),
        lax.psum(up_bias_grad.astype(jnp.bfloat16), "dp").astype(jnp.float32),
        lax.psum(down_weight_grad.astype(jnp.bfloat16), "dp").astype(jnp.float32),
    )
    norms = lax.psum(
        (
            attention_gain_gradient,
            first_bias_grad,
            feedforward_gain_gradient,
            second_bias_grad,
            down_bias_grad,
        ),
        ("dp", "mp"),
    )
    return (
        output,
        tokens_grad,
        norms[0],
        norms[1],
        summed[0],
        summed[1],
        summed[2],
        summed[3],
        norms[2],
        norms[3],
        summed[4],
        summed[5],
        summed[6],
        norms[4],
        new_memory,
        new_compressed,
    )


def solution(mesh):
    in_specs = (
        P("dp", "mp", None),
        P("dp", "mp", None),
        P("dp", "mp", None),
        P("dp"),
        P(),
        P(),
        P(None, "mp"),
        P(None, "mp"),
        P(None, "mp"),
        P("mp", None),
        P(),
        P(),
        P(None, "mp"),
        P("mp"),
        P("mp", None),
        P(),
        P(),
        P("dp", "mp", None),
    )
    out_specs = (
        P("dp", "mp", None),
        P("dp", "mp", None),
        P(),
        P(),
        P(None, "mp"),
        P(None, "mp"),
        P(None, "mp"),
        P("mp", None),
        P(),
        P(),
        P(None, "mp"),
        P("mp"),
        P("mp", None),
        P(),
        P("dp", "mp", None),
        P("dp", "mp", None),
    )
    return jax.shard_map(
        per_device, mesh=mesh, in_specs=in_specs, out_specs=out_specs, check_vma=False
    )
```

profile of v0, /device:TPU:9, one launch (start us, length us, event | category | flops | bytes accessed | tf_op | source)
XLA Modules:
  0.0 850.1 jit_solution(12164202690082199267)
XLA Ops:
  12.8 42.1 %all-gather.9.cloned.1.call-done = bf16[2,512,1024]{2,1,0:T(8,128)(2,1)} async-done(((bf16[2,128,1024]{2,1,0:T(8,128)(2,1)}), bf16[2,512,1024]{2,1,0:T(8,128)(2,1)}) %all-gather.9.cloned.1.call-update) | async-done | bytes 2097168 | tf_op jit(solution)/shard_map/all_gather | solution.py:77
  54.9 46.3 %all-gather.7.cloned.1.call-done = bf16[2,512,1024]{2,1,0:T(8,128)(2,1)} async-done(((bf16[2,128,1024]{2,1,0:T(8,128)(2,1)}), bf16[2,512,1024]{2,1,0:T(8,128)(2,1)}) %all-gather.7.cloned.1.call-update) | async-done | bytes 2097168 | tf_op jit(solution)/shard_map/all_gather | solution.py:76
  101.1 46.3 %all-gather.11.cloned.1.call-done = bf16[2,512,1024]{2,1,0:T(8,128)(2,1)} async-done(((bf16[2,128,1024]{2,1,0:T(8,128)(2,1)}), bf16[2,512,1024]{2,1,0:T(8,128)(2,1)}) %all-gather.11.cloned.1.call-update) | async-done | bytes 2097168 | tf_op jit(solution)/shard_map/all_gather | solution.py:78
  147.4 4.9 convert_reduce_fusion
  152.4 5.4 fusion.2
  157.8 5.2 fusion.5
  176.7 4.5 fusion.59
  184.8 77.5 %reduce-scatter.5.cloned.1.call-done = f32[2,128,1024]{2,1,0:T(8,128)} async-done(((f32[2,512,1024]{2,1,0:T(8,128)}), f32[2,128,1024]{2,1,0:T(8,128)}) %reduce-scatter.5.cloned.1.call-update) | async-done | bytes 1048592 | tf_op jit(solution)/shard_map/reduce_scatter | solution.py:135
  265.8 44.1 %all-gather.13.cloned.1.call-done = bf16[2,512,1024]{2,1,0:T(8,128)(2,1)} async-done(((bf16[2,128,1024]{2,1,0:T(8,128)(2,1)}), bf16[2,512,1024]{2,1,0:T(8,128)(2,1)}) %all-gather.13.cloned.1.call-update) | async-done | bytes 2097168 | tf_op jit(solution)/shard_map/all_gather | solution.py:141
  309.9 6.6 fusion.34
  316.5 39.6 %all-gather.15.cloned.1.call-done = bf16[2,512,1024]{2,1,0:T(8,128)(2,1)} async-done(((bf16[2,128,1024]{2,1,0:T(8,128)(2,1)}), bf16[2,512,1024]{2,1,0:T(8,128)(2,1)}) %all-gather.15.cloned.1.call-update) | async-done | bytes 2097168 | tf_op jit(solution)/shard_map/all_gather | solution.py:164
  356.1 7.5 fusion.91
  369.3 77.5 %reduce-scatter.9.cloned.1.call-done = f32[2,128,1024]{2,1,0:T(8,128)} async-done(((f32[2,512,1024]{2,1,0:T(8,128)}), f32[2,128,1024]{2,1,0:T(8,128)}) %reduce-scatter.9.cloned.1.call-update) | async-done | bytes 1048592 | tf_op jit(solution)/shard_map/reduce_scatter | solution.py:179
  451.6 6.1 bitcast_convert_fusion.1
  462.1 33.7 %all-gather.17.cloned.1.call-done = bf16[2,512,1024]{2,1,0:T(8,128)(2,1)} async-done(((bf16[2,128,1024]{2,1,0:T(8,128)(2,1)}), bf16[2,512,1024]{2,1,0:T(8,128)(2,1)}) %all-gather.17.cloned.1.call-update) | async-done | bytes 2097168 | tf_op jit(solution)/shard_map/all_gather | solution.py:190
  498.3 7.0 fusion.26
  505.4 9.5 %multiply_reduce_fusion = (f32[2,2,512]{2,1,0:T(2,128)S(1)}, f32[2,2,512,1536]{3,2,1,0:T(8,128)}) fusion(f32[2,2,512,1536]{3,2,1,0:T(8,128)} %copy-done.1, f32[2,2,512]{2,1,0:T(2,128)S(1)} %log_add_fusion, bf16[2,512,2,128]{1,3,2,0:T(8,128)(2,1)S(1)} %bitcast.182, bf16[2,1536,2,128]{1,3,2,0:T(8,128)(2,1)S(1)} %bitcast.184), kind=kOutput, calls=%fused_computation.15 | convolution fusion | flops 814741504 | bytes 27279360 | tf_op jit(solution)/shard_map/gqhe,gkhe->ghqk/dot_general | solution.py:200
  514.9 6.4 multiply_convert_fusion
  537.6 7.2 convolution_add_fusion
  544.8 5.1 fusion.21
  549.9 8.4 convert_element_type.161
  558.3 6.9 copy.66
  569.1 6.4 fusion.36
  579.8 8.3 while.4
  591.7 6.4 fusion.49
  598.1 8.1 gather_fusion.1
  610.3 5.3 pad_maximum_fusion.1
  616.6 7.3 while.3
  623.9 12.5 %psum.93 = bf16[1024]{0:T(1024)(128)(2,1)S(1)} all-reduce(bf16[1024]{0:T(1024)(128)(2,1)S(1)} %get-tuple-element.121), channel_id=1, replica_groups=mesh['dp'=8,'mp'=4] {'dp'}, use_global_device_ids=true, to_apply=%region_31.32 | all-reduce | flops 1024 | bytes 4096 | tf_op jit(solution)/shard_map/psum | solution.py:269
  652.7 100.4 %reduce-scatter.11.cloned.1.call-done = bf16[2,3,128,1024]{3,2,0,1:T(8,128)(2,1)} async-done(((bf16[2,3,512,1024]{3,2,0,1:T(8,128)(2,1)}), bf16[2,3,128,1024]{3,2,0,1:T(8,128)(2,1)}) %reduce-scatter.11.cloned.1.call-update) | async-done | bytes 1572880 | tf_op jit(solution)/shard_map/reduce_scatter | solution.py:250
  758.0 39.4 %reduce-scatter.7.cloned.1.call-done = bf16[2,128,1024]{2,1,0:T(8,128)(2,1)} async-done(((bf16[2,512,1024]{2,1,0:T(8,128)(2,1)}), bf16[2,128,1024]{2,1,0:T(8,128)(2,1)}) %reduce-scatter.7.cloned.1.call-update) | async-done | bytes 524304 | tf_op jit(solution)/shard_map/reduce_scatter | solution.py:151
  801.4 41.7 %all-reduce.3 = (f32[1024]{0:T(1024)}, f32[1024]{0:T(1024)}, f32[1024]{0:T(1024)}, f32[1024]{0:T(1024)}, f32[1024]{0:T(1024)}) all-reduce(f32[1024]{0:T(1024)S(1)} %get-tuple-element.65, f32[1024]{0:T(1024)S(1)} %get-tuple-element.64, f32[1024]{0:T(1024)S(1)} %get-tuple-element.62, ...), channel_id=1, replica_groups=mesh['dp'=8,'mp'=4] {'dp','mp'}, use_global_device_ids=true, to_apply=%region_18.19 | all-reduce | flops 5120 | bytes 40960 | tf_op jit(solution)/shard_map/psum | solution.py:272
  (209 shorter events, 117.2 us)
Async XLA Ops:
  7.2 348.9 %copy-start = (bf16[1024,1024]{1,0:T(8,128)(2,1)S(1)}, bf16[1024,1024]{1,0:T(8,128)(2,1)}, u32[]{:S(2)}) copy-start(bf16[1024,1024]{1,0:T(8,128)(2,1)} %param.34) | copy-start | bytes 6291460
  7.2 47.7 %all-gather.9.cloned.1.call-start = ((), (), s32[]{:S(2)}) async-start(), calls=%async_computation.5 | async-start | bytes 2621440 | tf_op jit(solution)/shard_map/all_gather | solution.py:77
  7.9 93.2 %all-gather.7.cloned.1.call-start = ((), (), s32[]{:S(2)}) async-start(), calls=%async_computation.4 | async-start | bytes 2621440 | tf_op jit(solution)/shard_map/all_gather | solution.py:76
  8.7 138.7 %all-gather.11.cloned.1.call-start = ((), (), s32[]{:S(2)}) async-start(), calls=%async_computation.6 | async-start | bytes 2621440 | tf_op jit(solution)/shard_map/all_gather | solution.py:78
  9.4 252.9 %reduce-scatter.5.cloned.1.call-start = ((), (), s32[]{:S(2)}) async-start(), calls=%async_computation.7 | async-start | bytes 5242880 | tf_op jit(solution)/shard_map/reduce_scatter | solution.py:135
  152.3 5.5 copy-start.37
  152.3 5.5 copy-start.39
  157.8 6.0 copy-start.28
  184.7 79.4 %copy-start.36 = (f32[1024]{0:T(1024)S(1)}, f32[1024]{0:T(1024)}, u32[]{:S(2)}) copy-start(f32[1024]{0:T(1024)} %param.30) | copy-start | bytes 12292
  184.7 79.4 %copy-start.40 = (f32[1024]{0:T(1024)S(1)}, f32[1024]{0:T(1024)}, u32[]{:S(2)}) copy-start(f32[1024]{0:T(1024)} %param.31) | copy-start | bytes 12292
  184.8 125.1 %all-gather.13.cloned.1.call-start = ((), (), s32[]{:S(2)}) async-start(), calls=%async_computation.8 | async-start | bytes 2621440 | tf_op jit(solution)/shard_map/all_gather | solution.py:141
  265.2 90.9 %all-gather.15.cloned.1.call-start = ((), (), s32[]{:S(2)}) async-start(), calls=%async_computation.10 | async-start | bytes 2621440 | tf_op jit(solution)/shard_map/all_gather | solution.py:164
  265.8 90.3 %copy-start.46 = (f32[1024]{0:T(1024)S(1)}, f32[1024]{0:T(1024)}, u32[]{:S(2)}) copy-start(f32[1024]{0:T(1024)} %param.33) | copy-start | bytes 12292
  265.8 181.0 %reduce-scatter.9.cloned.1.call-start = ((), (), s32[]{:S(2)}) async-start(), calls=%async_computation.11 | async-start | bytes 5242880 | tf_op jit(solution)/shard_map/reduce_scatter | solution.py:179
  356.1 8.8 %copy-start.43 = (bf16[1024,1024]{1,0:T(8,128)(2,1)S(1)}, bf16[1024,1024]{1,0:T(8,128)(2,1)}, u32[]{:S(2)}) copy-start(bf16[1024,1024]{1,0:T(8,128)(2,1)} %param.32) | copy-start | bytes 6291460
  369.3 126.5 %all-gather.17.cloned.1.call-start = ((), (), s32[]{:S(2)}) async-start(), calls=%async_computation.12 | async-start | bytes 2621440 | tf_op jit(solution)/shard_map/all_gather | solution.py:190
  451.1 188.6 %all-reduce.7.cloned.1.call-start = ((), (), s32[]{:S(2)}) async-start(), calls=%async_computation.14 | async-start | bytes 12582912 | tf_op jit(solution)/shard_map/psum | solution.py:264
  451.6 6.1 copy-start.44
  451.6 6.1 copy-start.48
  498.3 7.1 copy-start.26
  498.3 16.6 %slice-start = ((s8[12582912]{0:T(1024)(128)(4,1)}), s8[4194304]{0:T(1024)(128)(4,1)S(1)}, s32[]{:S(2)}) async-start(s8[12582912]{0:T(1024)(128)(4,1)} %bitcast.155), calls=%async_computation.15 | async-start | bytes 8388608
  498.3 16.6 %slice-start.1 = ((s8[12582912]{0:T(1024)(128)(4,1)}), s8[4194304]{0:T(1024)(128)(4,1)S(1)}, s32[]{:S(2)}) async-start(s8[12582912]{0:T(1024)(128)(4,1)} %bitcast.155), calls=%async_computation.16 | async-start | bytes 8388608
  505.3 19.1 %copy-start.16 = (bf16[2,2,128,1536]{3,2,1,0:T(8,128)(2,1)}, bf16[2,2,128,1536]{3,2,1,0:T(8,128)(2,1)S(1)}, u32[]{:S(2)}) copy-start(bf16[2,2,128,1536]{3,2,1,0:T(8,128)(2,1)S(1)} %fusion.26) | copy-start | bytes 4718596
  505.3 9.5 %slice-start.2 = ((s8[12582912]{0:T(1024)(128)(4,1)}), s8[4194304]{0:T(1024)(128)(4,1)S(1)}, s32[]{:S(2)}) async-start(s8[12582912]{0:T(1024)(128)(4,1)} %bitcast.155), calls=%async_computation.17 | async-start | bytes 8388608
  514.9 6.4 copy-start.11
  533.7 219.4 %reduce-scatter.11.cloned.1.call-start = ((), (), s32[]{:S(2)}) async-start(), calls=%async_computation.13 | async-start | bytes 7864320 | tf_op jit(solution)/shard_map/reduce_scatter | solution.py:250
  537.5 7.2 copy-start.23
  537.5 7.2 copy-start.30
  565.1 232.3 %reduce-scatter.7.cloned.1.call-start = ((), (), s32[]{:S(2)}) async-start(), calls=%async_computation.9 | async-start | bytes 2621440 | tf_op jit(solution)/shard_map/reduce_scatter | solution.py:151
  639.7 6.4 copy-start.31
  639.7 7.5 copy-start.19
  755.4 42.0 %copy-start.41 = (f32[1024]{0:T(1024)S(1)}, f32[1024]{0:T(1024)}, u32[]{:S(2)}) copy-start(f32[1024]{0:T(1024)} %param.35) | copy-start | bytes 12292
  (33 other events, 107.0 us)
Sparse Core Ops, SparseCore 0:
  9.6 45.2 all-gather.8
  56.4 44.6 all-gather.6
  102.7 44.6 all-gather.10
  184.9 77.3 reduce-scatter.4
  265.3 44.5 all-gather.12
  311.4 44.6 all-gather.14
  369.4 77.3 reduce-scatter.8
  451.3 44.5 all-gather.16
  533.8 105.8 all-reduce.6
  642.0 111.0 reduce-scatter.10
  755.5 41.9 reduce-scatter.6
where the time goes:
time: 863 us; the launch traced here: 850 us
  waiting for transfers between devices  552 us (64%)
  matrix products  104 us (12%)
  other arithmetic  73.2 us (8%)
  blocking collectives  54.2 us (6%)
  local copies, waits for them, and re-layouts  49.8 us (6%)
  between operations  15.1 us (2%)
    reduce_scatter x1, waiting for transfers between devices, per_device(): lax.psum_scatter(partial_normed.astype(jnp.bfloat16), 'mp', scatter_dimen...  100 us
    reduce_scatter x1, waiting for transfers between devices, per_device(): lax.psum_scatter(partial_attn, 'mp', scatter_dimension=1, tiled=True)  77.5 us
    reduce_scatter x1, waiting for transfers between devices, per_device(): lax.psum_scatter(partial_second, 'mp', scatter_dimension=1, tiled=True)  77.5 us
    all_gather x1, waiting for transfers between devices, per_device(): lax.all_gather(tokens, 'mp', axis=1, tiled=True)  46.3 us
    all_gather x1, waiting for transfers between devices, per_device(): lax.all_gather(compressed, 'mp', axis=1, tiled=True)  46.3 us
    all_gather x1, waiting for transfers between devices, per_device(): second_all = lax.all_gather(feedforward_input, 'mp', axis=1, tiled=True)  44.1 us
    all_gather x1, waiting for transfers between devices, per_device(): lax.all_gather(memory, 'mp', axis=1, tiled=True)  42.1 us
    psum x1, blocking collectives, per_device(): lax.psum((attention_gain_gradient, first_bias_grad, feedforward_gain_grad...  41.7 us
  transfers between devices with their start and end apart: 11, of which 11 were waited for; matrix products, arithmetic and copies ran while one was open for 15% of the time, Pallas kernels for 0%

commit v1 on v0

--- a/solution.py
+++ b/solution.py
@@ -1,6 +1,10 @@
+import functools
+
 import jax
 import jax.numpy as jnp
 from jax import lax
+from jax.experimental import pallas as pl
+from jax.experimental.pallas import tpu as pltpu
 from jax.sharding import PartitionSpec as P
 
 HEAD_DIM = 128
@@ -50,7 +54,7 @@
     return (new_memory, new_compressed)
 
 
-def per_device(
+def general_device(
     tokens,
     memory,
     compressed,
@@ -299,6 +303,732 @@
     )
 
 
+BF = jnp.bfloat16
+F32 = jnp.float32
+MESH = pl.DeviceIdType.MESH
+ANY = pl.BlockSpec(memory_space=pl.ANY)
+VM = pl.BlockSpec(memory_space=pltpu.VMEM)
+DMA = pltpu.SemaphoreType.DMA
+
+
+def sds(shape, dtype):
+    return jax.ShapeDtypeStruct(shape, dtype)
+
+
+def where_am_i(chips, depth):
+    dp = lax.axis_index("dp")
+    return dp, lax.rem(dp, 2), dp // 2, lax.axis_index("mp")
+
+
+def rcopy(src, dst, send, recv, device):
+    return pltpu.make_async_remote_copy(
+        src_ref=src,
+        dst_ref=dst,
+        send_sem=send,
+        recv_sem=recv,
+        device_id=device,
+        device_id_type=MESH,
+    )
+
+
+def lcopy(src, dst, sem):
+    return pltpu.make_async_copy(src, dst, sem)
+
+
+def enter(partners):
+    barrier = pltpu.get_barrier_semaphore()
+    for p in partners:
+        pl.semaphore_signal(barrier, inc=1, device_id=p, device_id_type=MESH)
+    pl.semaphore_wait(barrier, len(partners))
+
+
+def gather_kernel(Q, Z, comp, mem, tok, cot, wq, wk, wv, wo, ub, vc, ctx, wqg, wkg, wvg, wog, ubg, vco,
+                  ws, wr, ps, pr, cs, cr, fs, fr, ls, us, ur, ms):
+    dp, c, q, z = where_am_i(Q, Z)
+    sib = dp + 1 - 2 * c
+    partners = [(sib, z)]
+    for r in range(1, Z):
+        for d in (dp, sib):
+            partners.append((d, lax.rem(z + r, Z)))
+    for k in range(1, Q):
+        partners.append((2 * lax.rem(q + k, Q) + c, z))
+    enter(partners)
+    B, R, D = tok.shape
+    H = wq.shape[1]
+    QR = wq.shape[0] // Q
+    OR = wo.shape[0] // Q
+    HR = R // 2
+    mine = c == z // B
+    weights = [(wq, wqg), (wk, wkg), (wv, wvg), (wo, wog)]
+    acts = [comp, mem, tok, cot]
+
+    def piece(a):
+        if a < 3:
+            return weights[a][0].at[pl.ds(q * QR, QR), :]
+        return wo.at[pl.ds(q * OR, OR), :]
+
+    def place(a, j, qq):
+        if a < 3:
+            return weights[a][1].at[j, pl.ds(qq * QR, QR), :]
+        return wog.at[j, pl.ds(qq * OR, OR), :]
+
+    def w_z(a, r):
+        zt = lax.rem(z + r, Z)
+        return rcopy(piece(a), place(a, lax.rem(z, B), q), ws.at[a, r - 1], wr.at[a, lax.rem(z, B)], (dp, zt))
+
+    def u_z(r):
+        return rcopy(ub.at[dp], ubg.at[r], us.at[r - 1], ur.at[r - 1], (dp, lax.rem(z + r, Z)))
+
+    v_s = rcopy(vc, vco, ms.at[0], ms.at[1], (sib, z))
+    u_l = lcopy(ub.at[dp], ubg.at[0], ls.at[0])
+
+    def w_l(a):
+        return lcopy(weights[a][0], weights[a][1].at[lax.rem(z, B)], ls.at[1 + a])
+
+    def c_l(t):
+        return lcopy(acts[t].at[lax.rem(z, B)], ctx.at[t, pl.ds(z * R, R), :], ls.at[5 + t])
+
+    def c_sib(t):
+        return rcopy(acts[t].at[lax.rem(z, B)], ctx.at[t, pl.ds(z * R, R), :], fs.at[t, z], fr.at[t, z], (sib, z))
+
+    def c_z(t, s, h):
+        return rcopy(
+            acts[t].at[s, pl.ds(HR * h, HR), :],
+            ctx.at[t, pl.ds(z * R + HR * h, HR), :],
+            cs.at[t, s, h],
+            cr.at[t, z],
+            (2 * q + h, B * c + s),
+        )
+
+    def c_arrive(t, zs):
+        rows = ctx.at[t, pl.ds(zs * R + HR * c, HR), :]
+        return rcopy(rows, rows, cs.at[t, 0, 0], cr.at[t, zs], (dp, z))
+
+    def c_fwd(t, zs, half):
+        rows = ctx.at[t, pl.ds(zs * R + HR * half, HR), :]
+        return rcopy(rows, rows, fs.at[t, zs], fr.at[t, zs], (sib, z))
+
+    def w_arrive(a, j):
+        return rcopy(place(a, j, q), place(a, j, q), ws.at[a, 0], wr.at[a, j], (dp, z))
+
+    def w_p(a, j, k, qq):
+        return rcopy(
+            place(a, j, qq), place(a, j, qq), ps.at[a, j, k - 1], pr.at[a, j, k - 1], (2 * lax.rem(q + k, Q) + c, z)
+        )
+
+    @pl.when(mine)
+    def _():
+        for a in range(4):
+            for r in range(1, Z):
+                w_z(a, r).start()
+    for r in range(1, Z):
+        u_z(r).start()
+    v_s.start()
+    u_l.start()
+
+    @pl.when(mine)
+    def _():
+        for a in range(4):
+            w_l(a).start()
+        for t in range(4):
+            c_l(t).start()
+            c_sib(t).start()
+    for j in range(B):
+        @pl.when(B * c + j != z)
+        def _():
+            for a in range(4):
+                w_arrive(a, j).wait_recv()
+                for k in range(1, Q):
+                    w_p(a, j, k, q).start()
+    for s in range(B):
+        @pl.when(B * c + s != z)
+        def _():
+            for t in range(4):
+                for h in range(2):
+                    c_z(t, s, h).start()
+    for zs in range(Z):
+        @pl.when(zs != z)
+        def _():
+            for t in range(4):
+                c_arrive(t, zs).wait_recv()
+                c_fwd(t, zs, c).start()
+    for zs in range(Z):
+        @pl.when(zs != z)
+        def _():
+            for t in range(4):
+                c_fwd(t, zs, 1 - c).wait_recv()
+                c_fwd(t, zs, c).wait_send()
+
+    @pl.when(mine)
+    def _():
+        for a in range(4):
+            w_l(a).wait()
+            for r in range(1, Z):
+                w_z(a, r).wait_send()
+        for t in range(4):
+            c_l(t).wait()
+            c_sib(t).wait_send()
+
+    @pl.when(jnp.logical_not(mine))
+    def _():
+        for t in range(4):
+            rows = ctx.at[t, pl.ds(z * R, R), :]
+            rcopy(rows, rows, fs.at[t, z], fr.at[t, z], (sib, z)).wait_recv()
+    for j in range(B):
+        @pl.when(B * c + j != z)
+        def _():
+            for a in range(4):
+                for k in range(1, Q):
+                    w_p(a, j, k, q).wait_send()
+                    w_p(a, j, k, lax.rem(q + Q - k, Q)).wait_recv()
+    for s in range(B):
+        @pl.when(B * c + s != z)
+        def _():
+            for t in range(4):
+                for h in range(2):
+                    c_z(t, s, h).wait_send()
+    for r in range(1, Z):
+        u_z(r).wait()
+    v_s.wait()
+    u_l.wait()
+
+
+def gather_inputs(Q, Z, comp, mem, tok, cot, wq, wk, wv, wo, ub, vc):
+    B, R, D = tok.shape
+    H = wq.shape[1]
+    return pl.pallas_call(
+        functools.partial(gather_kernel, Q, Z),
+        out_shape=[
+            sds((4, R * Z, D), BF),
+            sds((B, D, H), BF),
+            sds((B, D, H), BF),
+            sds((B, D, H), BF),
+            sds((B, H, D), BF),
+            sds((Z,) + ub.shape[1:], F32),
+            sds(vc.shape, jnp.int32),
+        ],
+        in_specs=[ANY] * 10,
+        out_specs=[ANY] * 7,
+        scratch_shapes=[
+            DMA((4, Z - 1)), DMA((4, B)),
+            DMA((4, B, Q - 1)), DMA((4, B, Q - 1)),
+            DMA((4, B, 2)), DMA((4, Z)),
+            DMA((4, Z)), DMA((4, Z)),
+            DMA((9,)),
+            DMA((Z - 1,)), DMA((Z - 1,)), DMA((2,)),
+        ],
+        compiler_params=pltpu.CompilerParams(collective_id=1, has_side_effects=True, vmem_limit_bytes=16 << 20),
+        name="gather_inputs",
+    )(comp, mem, tok, cot, wq, wk, wv, wo, ub, vc)
+
+
+def layer_norm_rows(rows):
+    center = jnp.mean(rows, axis=-1, keepdims=True)
+    centered = rows - center
+    spread = jnp.mean(centered * centered, axis=-1, keepdims=True)
+    inv = lax.rsqrt(spread + 1e-05)
+    return centered * inv, inv
+
+
+def second_kernel(Q, part, tok, gain, bias, resid, sec, got, own, ss, sr, ps, pr, fs, fr, ls):
+    dp, c, q, z = where_am_i(Q, 1)
+    sib = dp + 1 - 2 * c
+    enter([(sib, z)] + [(2 * lax.rem(q + k, Q) + c, z) for k in range(1, Q)])
+    N = own.shape[0]
+    parts = ss.shape[0]
+    C = N // parts
+
+    def s_x(i):
+        return rcopy(part.at[pl.ds((1 - c) * N + i * C, C), :], got.at[pl.ds(i * C, C), :], ss.at[i], sr.at[i], (sib, z))
+
+    def p_x(i, k):
+        return rcopy(
+            own.at[pl.ds(i * C, C), :], sec.at[k, 0, pl.ds(i * C, C), :], ps.at[i, k], pr.at[i, k], (2 * lax.rem(q + k, Q) + c, z)
+        )
+
+    def f_x(i, k):
+        src = own.at[pl.ds(i * C, C), :] if k == 0 else sec.at[k, 0, pl.ds(i * C, C), :]
+        return rcopy(src, sec.at[k, 1, pl.ds(i * C, C), :], fs.at[i, k], fr.at[i, k], (sib, z))
+
+    def l_x(i):
+        return lcopy(own.at[pl.ds(i * C, C), :], sec.at[0, 0, pl.ds(i * C, C), :], ls.at[i])
+
+    for i in range(parts):
+        s_x(i).start()
+    for i in range(parts):
+        s_x(i).wait_recv()
+        at = pl.multiple_of(c * N + i * C, C)
+        r = tok[pl.ds(at, C), :].astype(F32) + (part[pl.ds(at, C), :] + got[pl.ds(i * C, C), :])
+        resid[pl.ds(i * C, C), :] = r
+        xhat, _ = layer_norm_rows(r)
+        own[pl.ds(i * C, C), :] = (xhat * gain[...] + bias[...]).astype(BF)
+        for k in range(1, Q):
+            p_x(i, k).start()
+        f_x(i, 0).start()
+        l_x(i).start()
+    for i in range(parts):
+        for k in range(1, Q):
+            p_x(i, k).wait_recv()
+            f_x(i, k).start()
+    for i in range(parts):
+        s_x(i).wait_send()
+        l_x(i).wait()
+        for k in range(1, Q):
+            p_x(i, k).wait_send()
+        for k in range(Q):
+            f_x(i, k).wait()
+
+
+def second_rows(Q, part, tok, gain, bias, parts=2):
+    rows, D = part.shape
+    N = rows // 2
+    return pl.pallas_call(
+        functools.partial(second_kernel, Q),
+        out_shape=[sds((N, D), F32), sds((Q, 2, N, D), BF)],
+        in_specs=[VM] * 4,
+        out_specs=[VM, ANY],
+        scratch_shapes=[
+            pltpu.VMEM((N, D), F32), pltpu.VMEM((N, D), BF),
+            DMA((parts,)), DMA((parts,)), DMA((parts, Q)), DMA((parts, Q)), DMA((parts, Q)), DMA((parts, Q)), DMA((parts,)),
+        ],
+        compiler_params=pltpu.CompilerParams(collective_id=2, has_side_effects=True, vmem_limit_bytes=32 << 20),
+        name="second_rows",
+    )(part, tok, gain, bias)
+
+
+def resid_kernel(Q, part, resid, cot, gain, grad, all_low, sums, got1, send2, got2, low, ss, sr, ps, pr, fs, ls):
+    dp, c, q, z = where_am_i(Q, 1)
+    sib = dp + 1 - 2 * c
+    enter([(sib, z)] + [(2 * lax.rem(q + k, Q) + c, z) for k in range(1, Q)])
+    N, D = resid.shape
+
+    def s_x(k):
+        return rcopy(part.at[k, 1], got1.at[k], ss.at[k], sr.at[k], (sib, z))
+
+    def p_x(k):
+        return rcopy(send2.at[k - 1], got2.at[k - 1], ps.at[k - 1], pr.at[k - 1], (2 * lax.rem(q + Q - k, Q) + c, z))
+
+    order = list(range(1, Q)) + [0]
+    for k in order:
+        s_x(k).start()
+    for k in range(1, Q):
+        s_x(k).wait_recv()
+        send2[k - 1] = (part[k, 0].astype(F32) + got1[k].astype(F32)).astype(BF)
+        p_x(k).start()
+    s_x(0).wait_recv()
+    for k in range(1, Q):
+        p_x(k).wait_recv()
+    g_gain = jnp.zeros((1, D), F32)
+    g_bias = jnp.zeros((1, D), F32)
+    C = 64
+    for i in range(N // C):
+        at = pl.ds(i * C, C)
+        gs = part[0, 0, at, :].astype(F32) + got1[0, at, :].astype(F32)
+        for k in range(1, Q):
+            gs = gs + got2[k - 1, at, :].astype(F32)
+        xhat, inv = layer_norm_rows(resid[at, :])
+        g_gain = g_gain + jnp.sum(gs * xhat, axis=0, keepdims=True)
+        g_bias = g_bias + jnp.sum(gs, axis=0, keepdims=True)
+        e = gs * gain[...]
+        m1 = jnp.mean(e, axis=-1, keepdims=True)
+        m2 = jnp.mean(e * xhat, axis=-1, keepdims=True)
+        gr = cot[at, :].astype(F32) + inv * (e - m1 - xhat * m2)
+        grad[at, :] = gr
+        low[at, :] = gr.astype(BF)
+    sums[0:1, :] = g_gain
+    sums[1:2, :] = g_bias
+    far = rcopy(low, all_low.at[pl.ds(c * N, N), :], fs.at[0], fs.at[1], (sib, z))
+    near = lcopy(low, all_low.at[pl.ds(c * N, N), :], ls.at[0])
+    far.start()
+    near.start()
+    for k in range(Q):
+        s_x(k).wait_send()
+    for k in range(1, Q):
+        p_x(k).wait_send()
+    near.wait()
+    far.wait()
+
+
+def resid_grads(Q, part, resid, cot, gain):
+    N, D = resid.shape
+    return pl.pallas_call(
+        functools.partial(resid_kernel, Q),
+        out_shape=[sds((N, D), F32), sds((2 * N, D), BF), sds((2, D), F32)],
+        in_specs=[VM] * 4,
+        out_specs=[VM, ANY, VM],
+        scratch_shapes=[
+            pltpu.VMEM((Q, N, D), BF), pltpu.VMEM((Q - 1, N, D), BF), pltpu.VMEM((Q - 1, N, D), BF), pltpu.VMEM((N, D), BF),
+            DMA((Q,)), DMA((Q,)), DMA((Q - 1,)), DMA((Q - 1,)), DMA((2,)), DMA((1,)),
+        ],
+        compiler_params=pltpu.CompilerParams(collective_id=3, has_side_effects=True, vmem_limit_bytes=40 << 20),
+        name="resid_grads",
+    )(part, resid, cot, gain)
+
+
+def final_kernel(Q, Z, B, gq, gk, gv, go, fu, fd, r0, r1, r2, r3, agq, agk, agv, ago, afu, afd, o0, o1, o2, o3,
+                 bq, bk, bv, bo, zq, zk, zv, zo, dq, dk, dv, do, ps, pr, zs_, zr, gs_, gr, hs, hr, us, ur, vs, vr, ls, rs, rr):
+    dp, c, q, z = where_am_i(Q, Z)
+    sib = dp + 1 - 2 * c
+    partners = [(sib, z)]
+    for r in range(1, Z):
+        for d in (dp, sib):
+            partners.append((d, lax.rem(z + r, Z)))
+    for k in range(1, Q):
+        partners.append((2 * lax.rem(q + k, Q) + c, z))
+    enter(partners)
+    grads = [gq, gk, gv, go]
+    bufs = [bq, bk, bv, bo]
+    zbufs = [zq, zk, zv, zo]
+    done = [dq, dk, dv, do]
+    outs = [agq, agk, agv, ago]
+    rows_in = [r0, r1, r2, r3]
+    rows_out = [o0, o1, o2, o3]
+    M = agq.shape[0] // Q
+    OM = ago.shape[0] // Q
+    RR = o0.shape[1]
+    mine = c == z // B
+    jz = lax.rem(z, B)
+    zc = z // B
+
+    def quarter(a, qq):
+        n = OM if a == 3 else M
+        return grads[a].at[:, pl.ds(qq * n, n), :]
+
+    def p_x(a, k):
+        return rcopy(quarter(a, lax.rem(q + k, Q)), bufs[a].at[k - 1], ps.at[a, k - 1], pr.at[a, k - 1],
+                     (2 * lax.rem(q + k, Q) + c, z))
+
+    def z_x(a, j):
+        return rcopy(done[a].at[j], zbufs[a].at[z], zs_.at[a, j], zr.at[a, z], (dp, B * c + j))
+
+    def z_arrive(a, zz):
+        return rcopy(zbufs[a].at[zz], zbufs[a].at[zz], zs_.at[a, 0], zr.at[a, zz], (dp, z))
+
+    def where_out(a, qq):
+        n = OM if a == 3 else M
+        return outs[a].at[pl.ds(qq * n, n), :]
+
+    def f_out(i, d):
+        return (afu if i == 0 else afd).at[d]
+
+    def u_x(i, k):
+        src = (fu, fd)[i]
+        return rcopy(src, f_out(i, dp), us.at[i, k], ur.at[i, k], (2 * lax.rem(q + k, Q) + c, z))
+
+    def v_x(i, k, d):
+        src = (fu, fd)[i] if k == 0 else f_out(i, d)
+        return rcopy(src, f_out(i, d), vs.at[i, k], vr.at[i, k], (sib, z))
+
+    def u_l(i):
+        return lcopy((fu, fd)[i], f_out(i, dp), ls.at[i])
+
+    per = r0.shape[0] // RR
+
+    def row_x(i, p):
+        zt = c * per + p
+        return rcopy(rows_in[i].at[pl.ds(p * RR, RR), :], rows_out[i].at[jz], rs.at[i, p], rr.at[i, jz], (2 * q + zc, zt))
+
+    def row_l(i, p):
+        return lcopy(rows_in[i].at[pl.ds(p * RR, RR), :], rows_out[i].at[jz], ls.at[2 + i])
+
+    for a in range(4):
+        for k in range(1, Q):
+            p_x(a, k).start()
+    for p in range(per):
+        here = (c * per + p == z) & mine
+        @pl.when(here)
+        def _():
+            for i in range(4):
+                row_l(i, p).start()
+
+        @pl.when(jnp.logical_not(here))
+        def _():
+            for i in range(4):
+                row_x(i, p).start()
+    for i in range(2):
+        for k in range(1, Q):
+            u_x(i, k).start()
+        v_x(i, 0, dp).start()
+        u_l(i).start()
+    for a in range(4):
+        n = OM if a == 3 else M
+        for k in range(1, Q):
+            p_x(a, k).wait_recv()
+        for j in range(B):
+            t = grads[a][j, pl.ds(pl.multiple_of(q * n, n), n), :].astype(F32)
+            for k in range(1, Q):
+                t = t + bufs[a][k - 1, j].astype(F32)
+            done[a][j] = t.astype(BF)
+
+            @pl.when(B * c + j != z)
+            def _():
+                z_x(a, j).start()
+    @pl.when(mine)
+    def _():
+        for a in range(4):
+            for zz in range(Z):
+                @pl.when(zz != z)
+                def _():
+                    z_arrive(a, zz).wait_recv()
+    for a in range(4):
+        @pl.when(mine)
+        def _():
+            zbufs[a][z] = done[a][jz]
+            t = zbufs[a][0].astype(F32)
+            for zz in range(1, Z):
+                t = t + zbufs[a][zz].astype(F32)
+            n = OM if a == 3 else M
+            outs[a][pl.ds(pl.multiple_of(q * n, n), n), :] = t.astype(BF)
+
+    def g_x(a, k):
+        return rcopy(where_out(a, q), where_out(a, q), gs_.at[a, k], gr.at[a, k], (2 * lax.rem(q + k, Q) + c, z))
+
+    def h_x(a, k):
+        qq = lax.rem(q + Q - k, Q)
+        return rcopy(where_out(a, qq), where_out(a, qq), hs.at[a, k], hr.at[a, k], (sib, z))
+
+    @pl.when(mine)
+    def _():
+        for a in range(4):
+            for k in range(1, Q):
+                g_x(a, k).start()
+            h_x(a, 0).start()
+    for i in range(2):
+        for k in range(1, Q):
+            u_x(i, k).wait_recv()
+            v_x(i, k, 2 * lax.rem(q + Q - k, Q) + c).start()
+
+    @pl.when(mine)
+    def _():
+        for a in range(4):
+            for k in range(1, Q):
+                g_x(a, k).wait_recv()
+                h_x(a, k).start()
+
+    @pl.when(mine)
+    def _():
+        for a in range(4):
+            for k in range(1, Q):
+                g_x(a, k).wait_send()
+            for k in range(Q):
+                h_x(a, k).wait_send()
+
+    @pl.when(jnp.logical_not(mine))
+    def _():
+        for a in range(4):
+            for k in range(Q):
+                h_x(a, k).wait_recv()
+    for a in range(4):
+        for k in range(1, Q):
+            p_x(a, k).wait_send()
+        for j in range(B):
+            @pl.when(B * c + j != z)
+            def _():
+                z_x(a, j).wait_send()
+    for i in range(2):
+        for k in range(1, Q):
+            u_x(i, k).wait_send()
+        for k in range(Q):
+            v_x(i, k, dp).wait_send()
+            v_x(i, k, dp).wait_recv()
+        u_l(i).wait()
+    for p in range(per):
+        here = (c * per + p == z) & mine
+        @pl.when(here)
+        def _():
+            for i in range(4):
+                row_l(i, p).wait()
+
+        @pl.when(jnp.logical_not(here))
+        def _():
+            for i in range(4):
+                row_x(i, p).wait_send()
+    for s in range(B):
+        @pl.when(jnp.logical_not((B * c + s == z) & mine))
+        def _():
+            for i in range(4):
+                rcopy(rows_out[i].at[s], rows_out[i].at[s], rs.at[i, 0], rr.at[i, s], (dp, z)).wait_recv()
+
+
+def final_exchange(Q, Z, gq, gk, gv, go, fu, fd, r0, r1, r2, r3):
+    B, D, H = gq.shape
+    RR = r0.shape[0] * 2 // Z
+    M, OM = D // Q, H // Q
+    qs, os_ = (M, H), (OM, D)
+    return pl.pallas_call(
+        functools.partial(final_kernel, Q, Z, B),
+        out_shape=[sds((D, H), BF)] * 3 + [sds((H, D), BF)]
+        + [sds((2 * Q,) + fu.shape, BF), sds((2 * Q,) + fd.shape, BF)]
+        + [sds((B, RR, D), BF)] * 4,
+        in_specs=[VM] * 4 + [ANY] * 6,
+        out_specs=[VM] * 4 + [ANY] * 6,
+        scratch_shapes=[pltpu.VMEM((Q - 1, B) + qs, BF)] * 3 + [pltpu.VMEM((Q - 1, B) + os_, BF)]
+        + [pltpu.VMEM((Z,) + qs, BF)] * 3 + [pltpu.VMEM((Z,) + os_, BF)]
+        + [pltpu.VMEM((B,) + qs, BF)] * 3 + [pltpu.VMEM((B,) + os_, BF)]
+        + [
+            DMA((4, Q - 1)), DMA((4, Q - 1)), DMA((4, B)), DMA((4, Z)),
+            DMA((4, Q)), DMA((4, Q)), DMA((4, Q)), DMA((4, Q)),
+            DMA((2, Q)), DMA((2, Q)), DMA((2, Q)), DMA((2, Q)), DMA((6,)), DMA((4, 2)), DMA((4, B)),
+        ],
+        compiler_params=pltpu.CompilerParams(collective_id=4, has_side_effects=True, vmem_limit_bytes=40 << 20),
+        name="final_exchange",
+    )(gq, gk, gv, go, fu, fd, r0, r1, r2, r3)
+
+
+def chip_device(Q, Z, tokens, memory, compressed, valid_counts, attention_norm_gain, attention_norm_bias,
+                query_projection, key_projection, value_projection, out_weight, feedforward_norm_gain,
+                feedforward_norm_bias, up_weight, up_bias, down_weight, down_bias, squeeze_weight, cotangent):
+    B, R, D = tokens.shape
+    H = query_projection.shape[1]
+    FL = up_weight.shape[1]
+    dp = lax.axis_index("dp")
+    z = lax.axis_index("mp")
+    c = lax.rem(dp, 2)
+    S = R * Z
+    N = S // 2
+    E = FL // (2 * Q)
+    jz = lax.rem(z, B)
+
+    def turn_z(a, r):
+        return lax.ppermute(a, "mp", [(i, (i + r) % Z) for i in range(Z)])
+
+    def turn_q(a, k):
+        return lax.ppermute(a, "dp", [(2 * i + s, 2 * ((i + k) % Q) + s) for i in range(Q) for s in range(2)])
+
+    def swap(a):
+        return lax.ppermute(a, "dp", [(i, i ^ 1) for i in range(2 * Q)])
+
+    ctx, wqg, wkg, wvg, wog, ubg, vco = gather_inputs(
+        Q, Z, compressed, memory, tokens, cotangent, query_projection, key_projection, value_projection, out_weight,
+        up_bias.reshape(2 * Q, 1, E), jnp.broadcast_to(valid_counts[:, None, None], (B, 8, 128)),
+    )
+    counts = jnp.where(c == z // B, valid_counts, vco[:, 0, 0])
+    count = jnp.where(jz == 0, counts[0], counts[1])
+    up_own = lax.dynamic_slice_in_dim(up_weight, dp * E, E, 1)
+    down_own = lax.dynamic_slice_in_dim(down_weight, dp * E, E, 0)
+    up_loc = jnp.concatenate([up_own] + [turn_z(up_own, r) for r in range(1, Z)], axis=1)
+    down_loc = jnp.concatenate([down_own] + [turn_z(down_own, r) for r in range(1, Z)], axis=0)
+    ub_loc = ubg.reshape(Z * E)
+    cot_own = lax.dynamic_slice_in_dim(ctx[3], c * N, N, 0)
+    cot_q = jnp.stack([cot_own] + [turn_q(cot_own, k) for k in range(1, Q)])
+    cot_all = jnp.stack([cot_q, swap(cot_q)], axis=1).reshape(2 * Q * N, D)
+
+    rows = ctx[:3].reshape(3 * S, D).astype(F32)
+    xhat1, inv1 = layer_norm_rows(rows)
+    normed = (xhat1 * attention_norm_gain + attention_norm_bias).astype(BF)
+    nt = normed[2 * S:]
+    q_ = jnp.einsum("sd,jdh->sjh", nt, wqg, preferred_element_type=F32).astype(BF)
+    k_ = jnp.einsum("sd,jdh->sjh", normed, wkg, preferred_element_type=F32).astype(BF)
+    v_ = jnp.einsum("sd,jdh->sjh", normed, wvg, preferred_element_type=F32).astype(BF)
+    heads = B * H // HEAD_DIM
+
+    def by_heads(m):
+        return m.reshape(m.shape[0], heads, HEAD_DIM)
+
+    scale = HEAD_DIM ** (-0.5)
+    qpos = jnp.arange(S)[:, None]
+    kpos = jnp.arange(3 * S)[None, :] - 2 * S
+    allowed = (kpos < 0) | ((kpos <= qpos) & (kpos < count))
+
+    def scores_of():
+        raw = jnp.einsum("qhe,khe->hqk", by_heads(q_), by_heads(k_), preferred_element_type=F32) * scale
+        return jnp.where(allowed[None], raw, -1e30)
+
+    scores = scores_of()
+    peak = jnp.max(scores, axis=-1, keepdims=True)
+    expo = jnp.exp(scores - peak)
+    total = jnp.sum(expo, axis=-1, keepdims=True)
+    log_total = peak + jnp.log(total)
+    probs_low = (expo / total).astype(BF)
+    mixed = jnp.einsum("hqk,khe->qhe", probs_low, by_heads(v_), preferred_element_type=F32).astype(BF)
+    mixed = mixed.reshape(S, B, H)
+    part = jnp.einsum("sjh,jhd->sd", mixed, wog, preferred_element_type=F32)
+    resid, sec = second_rows(Q, part, ctx[2], feedforward_norm_gain.reshape(1, D), feedforward_norm_bias.reshape(1, D))
+    sec = sec.reshape(2 * Q * N, D)
+    upper = jnp.dot(sec, up_loc, preferred_element_type=F32) + ub_loc
+    active, gelu_back = jax.vjp(jax.nn.gelu, upper)
+    active = active.astype(BF)
+    g_active = lax.dot_general(cot_all, down_loc, (((1,), (1,)), ((), ())), preferred_element_type=F32)
+    g_upper = gelu_back(g_active)[0].astype(BF)
+    g_sec = lax.dot_general(g_upper, up_loc, (((1,), (1,)), ((), ())), preferred_element_type=F32)
+    g_sec = g_sec.astype(BF).reshape(Q, 2, N, D)
+    g_resid, g_low, ff_sums = resid_grads(Q, g_sec, resid, cot_own, feedforward_norm_gain.reshape(1, D))
+    down = jnp.dot(active, down_loc, preferred_element_type=F32).astype(BF).reshape(Q, 2, N, D)
+    down_half = down[:, 0].astype(F32) + swap(down[:, 1]).astype(F32)
+    down_low = down_half.astype(BF)
+    down_sum = down_half[0]
+    for k in range(1, Q):
+        down_sum = down_sum + turn_q(down_low[k], Q - k).astype(F32)
+    output = (resid + down_sum + down_bias).astype(BF)
+    up_grad = lax.dot_general(sec, g_upper, (((0,), (0,)), ((), ())), preferred_element_type=F32)
+    down_grad = lax.dot_general(active, cot_all, (((0,), (0,)), ((), ())), preferred_element_type=F32)
+    ub_grad = jnp.sum(g_upper.astype(F32), axis=0).reshape(Z, E)
+    fu = up_grad[:, :E]
+    fd = down_grad[:E]
+    up_low, down_g_low = up_grad.astype(BF), down_grad.astype(BF)
+    for r in range(1, Z):
+        fu = fu + turn_z(up_low[:, r * E:(r + 1) * E], Z - r).astype(F32)
+        fd = fd + turn_z(down_g_low[r * E:(r + 1) * E], Z - r).astype(F32)
+
+    go = jnp.einsum("sjh,sd->jhd", mixed, g_low, preferred_element_type=F32).astype(BF)
+    g_mixed = jnp.einsum("sd,jhd->sjh", g_low, wog, preferred_element_type=F32).astype(BF).reshape(S, B * H)
+    probs = jnp.exp(scores_of() - log_total)
+    g_probs = jnp.einsum("qhe,khe->hqk", by_heads(g_mixed), by_heads(v_), preferred_element_type=F32)
+    row_dot = jnp.sum(probs * g_probs, axis=-1, keepdims=True)
+    g_scores = (probs * (g_probs - row_dot)).astype(BF)
+    gq_ = (scale * jnp.einsum("hqk,khe->qhe", g_scores, by_heads(k_), preferred_element_type=F32)).astype(BF)
+    gk_ = (scale * jnp.einsum("hqk,qhe->khe", g_scores, by_heads(q_), preferred_element_type=F32)).astype(BF)
+    gv_ = jnp.einsum("hqk,qhe->khe", probs.astype(BF), by_heads(g_mixed), preferred_element_type=F32).astype(BF)
+    gq_, gk_, gv_ = (g.reshape(g.shape[0], B, H) for g in (gq_, gk_, gv_))
+    gwq = jnp.einsum("sd,sjh->jdh", nt, gq_, preferred_element_type=F32).astype(BF)
+    gwk = jnp.einsum("sd,sjh->jdh", normed, gk_, preferred_element_type=F32).astype(BF)
+    gwv = jnp.einsum("sd,sjh->jdh", normed, gv_, preferred_element_type=F32).astype(BF)
+    g_normed = jnp.einsum("sjh,jdh->sd", gk_, wkg, preferred_element_type=F32)
+    g_normed = g_normed + jnp.einsum("sjh,jdh->sd", gv_, wvg, preferred_element_type=F32)
+    g_normed = g_normed.at[2 * S:].add(jnp.einsum("sjh,jdh->sd", gq_, wqg, preferred_element_type=F32))
+    at_gain = jnp.sum(g_normed * xhat1, axis=0)
+    at_bias = jnp.sum(g_normed, axis=0)
+    keep = lax.dynamic_slice_in_dim(g_normed, 2 * S + c * N, N, 0)
+    give = lax.dynamic_slice_in_dim(g_normed, 2 * S + (1 - c) * N, N, 0)
+    gn = keep + swap(give)
+    xt = lax.dynamic_slice_in_dim(xhat1, 2 * S + c * N, N, 0)
+    it = lax.dynamic_slice_in_dim(inv1, 2 * S + c * N, N, 0)
+    e = gn * attention_norm_gain
+    tokens_grad = g_resid + it * (
+        e - jnp.mean(e, axis=-1, keepdims=True) - xt * jnp.mean(e * xt, axis=-1, keepdims=True)
+    )
+
+    new_memory = lax.dynamic_slice_in_dim(ctx[1:3].reshape(2 * S, D), count + c * N, N, 0)
+    groups = S // RATE
+    squeezed = jnp.zeros((groups, D), F32)
+    for r in range(RATE):
+        pick = (jnp.arange(groups)[:, None] * RATE + r == jnp.arange(S)[None, :]).astype(BF)
+        picked = jnp.dot(pick, ctx[1], preferred_element_type=F32).astype(BF)
+        squeezed = squeezed + jnp.dot(picked, squeeze_weight[r * D:(r + 1) * D], preferred_element_type=F32)
+    stacked = jnp.concatenate([ctx[0], squeezed.astype(BF), jnp.zeros((8, D), BF)], axis=0)
+    new_compressed = lax.dynamic_slice_in_dim(stacked, count // RATE + c * N, N, 0)
+
+    agq, agk, agv, ago, afu, afd, o_out, o_tg, o_nm, o_nc = final_exchange(
+        Q, Z, gwq, gwk, gwv, go, fu.astype(BF), fd.astype(BF), output, tokens_grad.astype(BF), new_memory, new_compressed
+    )
+    local_down_bias = jnp.sum(cotangent.astype(F32), axis=(0, 1))
+    ub_slots = jnp.zeros((Z, 2 * Q, E), F32)
+    for r in range(Z):
+        ub_slots = lax.dynamic_update_slice(ub_slots, ub_grad[r].reshape(1, 1, E), (lax.rem(z + Z - r, Z), dp, 0))
+    small = jnp.concatenate([
+        jnp.stack([at_gain, at_bias, ff_sums[0], ff_sums[1], local_down_bias]).reshape(-1), ub_slots.reshape(-1)
+    ])
+    small = lax.psum(small, ("dp", "mp"))
+    vecs = small[:5 * D].reshape(5, D)
+    ub_out = lax.dynamic_slice_in_dim(small[5 * D:], z * FL, FL, 0)
+    up_out = jnp.swapaxes(afu, 0, 1).reshape(D, FL).astype(F32)
+    down_out = afd.reshape(FL, D).astype(F32)
+    return (
+        o_out, o_tg.astype(F32), vecs[0], vecs[1], agq.astype(F32), agk.astype(F32), agv.astype(F32), ago.astype(F32),
+        vecs[2], vecs[3], up_out, ub_out, down_out, vecs[4], o_nm, o_nc,
+    )
+
+
 def solution(mesh):
     in_specs = (
         P("dp", "mp", None),
@@ -338,6 +1068,16 @@
         P("dp", "mp", None),
         P("dp", "mp", None),
     )
+    Q, Z = mesh.shape["dp"] // 2, mesh.shape["mp"]
+
+    def per_device(*args):
+        B, R, D = args[0].shape
+        H, FL = args[6].shape[1], args[12].shape[1]
+        whole = B == 2 and 2 * B == Z and H % HEAD_DIM == 0 and D % (16 * Q) == 0 and H % (16 * Q) == 0
+        if whole and R % 32 == 0 and FL % (256 * Q) == 0:
+            return chip_device(Q, Z, *args)
+        return general_device(*args)
+
     return jax.shard_map(
         per_device, mesh=mesh, in_specs=in_specs, out_specs=out_specs, check_vma=False
     )

time: 863 us -> 555 us (0.64)
  waiting for transfers between devices: 552 us -> 27.4 us
  Pallas kernels: 0 us -> 253 us
  matrix products: 104 us -> 80.9 us
  starting transfers between devices: 1.31 us -> 22.5 us
  blocking collectives: 54.2 us -> 39.7 us
  other arithmetic: 73.2 us -> 58.8 us
  between operations: 15.1 us -> 3.16 us
  local copies, waits for them, and re-layouts: 49.8 us -> 60.2 us
    reduce_scatter x4 -> x0, waiting for transfers between devices: 295 us -> none  [the longest x1 100 us: per_device(): lax.psum_scatter(partial_normed.astype(jnp.bfloat16), 'mp', scatter_dimen...]
    pallas_call x0 -> x4, Pallas kernels: none -> 253 us  [the longest x1 100 us: gather_inputs(): pl.pallas_call(functools.partial(gather_kernel, Q, Z), out_shape=[sds((4,...]
    all_gather x6 -> x0, waiting for transfers between devices: 252 us -> none  [the longest x1 46.3 us: per_device(): lax.all_gather(tokens, 'mp', axis=1, tiled=True)]
    gather x14 -> x0, local copies, waits for them, and re-layouts: 27.7 us -> none
    ppermute x0 -> x21, waiting for transfers between devices: none -> 27.4 us  [the longest x6 16.7 us: turn_q(): lax.ppermute(a, 'dp', [(2 * i + s, 2 * ((i + k) % Q) + s) for i in range(...]
    unnamed x111 -> x155, local copies, waits for them, and re-layouts: 7.69 us -> 31.7 us
    dot_general x25 -> x27, matrix products: 104 us -> 80.9 us  [the longest x3 10.2 us: chip_device(): jnp.dot(picked, squeeze_weight[r * D:(r + 1) * D], preferred_element_type...]
    ppermute x0 -> x21, starting transfers between devices: none -> 22.5 us  [the longest x12 11.8 us: turn_z(): return lax.ppermute(a, 'mp', [(i, (i + r) % Z) for i in range(Z)])]
  transfers between devices with their start and end apart: 11 -> 21, of which waited for: 11 -> 4; matrix products, arithmetic and copies ran while one was open for 15% -> 19% of each run, Pallas kernels for 0% -> 24%
where the time goes in v1:
time: 555 us; the launch traced here: 546 us
  Pallas kernels  253 us (46%)
  matrix products  80.9 us (15%)
  local copies, waits for them, and re-layouts  60.2 us (11%)
  other arithmetic  58.8 us (11%)
  blocking collectives  39.7 us (7%)
  waiting for transfers between devices  27.4 us (5%)
  starting transfers between devices  22.5 us (4%)
    pallas_call x1, Pallas kernels, gather_inputs(): pl.pallas_call(functools.partial(gather_kernel, Q, Z), out_shape=[sds((4,...  100 us
    pallas_call x1, Pallas kernels, final_exchange(): pl.pallas_call(functools.partial(final_kernel, Q, Z, B), out_shape=[sds((...  90.1 us
    psum x1, blocking collectives, chip_device(): small = lax.psum(small, ('dp', 'mp'))  39.7 us
    pallas_call x1, Pallas kernels, resid_grads(): pl.pallas_call(functools.partial(resid_kernel, Q), out_shape=[sds((N, D),...  32.2 us
    unnamed x155, local copies, waits for them, and re-layouts  31.7 us
    pallas_call x1, Pallas kernels, second_rows(): pl.pallas_call(functools.partial(second_kernel, Q), out_shape=[sds((N, D)...  30.6 us
    ppermute x6, waiting for transfers between devices, turn_q(): lax.ppermute(a, 'dp', [(2 * i + s, 2 * ((i + k) % Q) + s) for i in range(...  16.7 us
    ppermute x12, starting transfers between devices, turn_z(): return lax.ppermute(a, 'mp', [(i, (i + r) % Z) for i in range(Z)])  11.8 us
  transfers between devices with their start and end apart: 21, of which 4 were waited for; matrix products, arithmetic and copies ran while one was open for 19% of the time, Pallas kernels for 24%

profile of v1, /device:TPU:9, one launch (start us, length us, event | category | flops | bytes accessed | tf_op | source)
XLA Modules:
  0.0 546.0 jit_solution(17812173864585034088)
XLA Ops:
  20.2 100.4 %gather_inputs.1 = (bf16[4,512,1024]{2,1,0:T(8,128)(2,1)S(1)}, bf16[2,1024,256]{2,1,0:T(8,128)(2,1)S(1)}, bf16[2,1024,256]{2,1,0:T(8,128)(2,1)S(1)}, bf16[2,1024...) custom-call(bf16[2,128,1024]{2,1,0:T(8,128)(2,1)S(1)} %copy-done.25,, ...), custom_call_target="tpu_custom_call" | custom-call | tf_op jit(solution)/shard_map/gather_inputs/pallas_call | solution.py:499
  131.2 3.1 slice.172
  139.9 3.1 add_convert_fusion.1
  144.8 3.1 fusion.27
  147.9 3.1 fusion.24
  152.8 4.6 fusion.104
  162.1 3.7 fusion.41
  167.2 30.6 %second_rows.1 = (f32[256,1024]{1,0:T(8,128)S(1)}, bf16[4,2,256,1024]{3,2,1,0:T(8,128)(2,1)S(1)}) custom-call(f32[512,1024]{1,0:T(8,128)S(1)} %convolution_bitcast_fusion.part, bf16[512,1024]{1,0:T(8,128)(2,1)S(1)} %copy-done.7, f32[1,1024]{1,0:T(1,128)S(1)} %bitcast.186, f32[1,1024]{1,0:T(1,128)S(1)} %bitcast.189), custom_call_target="tpu_custom_call" | custom-call | tf_op jit(solution)/shard_map/second_rows/pallas_call | solution.py:585
  203.1 3.5 fusion.85
  208.9 4.1 convolution_convert_fusion
  217.5 3.6 fusion.33
  221.0 5.8 %collective-permute-done = bf16[256,1024]{1,0:T(8,128)(2,1)S(1)} collective-permute-done((bf16[256,1024]{1,0:T(8,128)(2,1)}, bf16[256,1024]{1,0:T(8,128)(2,1)S(1)}, u32[]{:S(2)}, u32[]{:S(2)}) %collective-permute-start) | collective-permute-done | bytes 524320 | tf_op jit(solution)/shard_map/ppermute | solution.py:896
  227.6 3.3 fusion.98
  232.9 3.6 fusion.31
  236.4 3.1 fusion.48
  242.0 4.0 add_convert_fusion
  246.1 4.6 fusion.96
  256.1 4.2 fusion.106
  260.3 6.5 %convert_reduce_fusion.1 = (f32[512]{0:T(512)S(1)}, bf16[2048,512]{1,0:T(8,128)(2,1)S(1)}) fusion(f32[2048,512]{1,0:T(8,128)S(1)} %copy-done.71, f32[512]{0:T(512)S(1)} %bitcast.192, bf16[2048,1024]{1,0:T(8,128)(2,1)S(1)} %bitcast.203, bf16[128,1024]{1,0:T(8,128)(2,1)} %collective-permute-done.6, bf16[128,1024]{1,0:T(8,128)(2,1)} %collective-permute-done.5, ...), kind=kOutput, calls=%fused_computation.31 | convolution fusion | flops 2175794688 | bytes 11538432 | tf_op jit(solution)/shard_map/dot_general | solution.py:951
  266.9 4.0 fusion.105
  270.9 3.9 convolution_convert_fusion.1
  274.8 32.2 %resid_grads.1 = (f32[256,1024]{1,0:T(8,128)S(1)}, bf16[512,1024]{1,0:T(8,128)(2,1)S(1)}, f32[2,1024]{1,0:T(2,128)S(1)}) custom-call(bf16[4,2,256,1024]{3,2,1,0:T(8,128)(2,1)S(1)} %bitcast.183, f32[256,1024]{1,0:T(8,128)S(1)} %get-tuple-element.58.resid, bf16[256,1024]{1,0:T(8,128)(2,1)} %fusion.142.cot, f32[1,1024]{1,0:T(1,128)S(1)} %bitcast.187), custom_call_target="tpu_custom_call" | custom-call | tf_op jit(solution)/shard_map/resid_grads/pallas_call | solution.py:654
  312.2 6.1 %multiply_reduce_fusion = (f32[4,512]{1,0:T(4,128)S(1)}, f32[4,512,1536]{2,1,0:T(8,128)}) fusion(f32[4,512,1536]{2,1,0:T(8,128)S(1)} %bitcast.194, f32[4,512]{1,0:T(4,128)S(1)} %log_add_fusion, bf16[512,4,128]{0,2,1:T(8,128)(2,1)S(1)} %bitcast.210, bf16[1536,4,128]{0,2,1:T(8,128)(2,1)S(1)} %bitcast.214), kind=kOutput, calls=%fused_computation.1 | convolution fusion | flops 814741504 | bytes 27279360 | tf_op jit(solution)/shard_map/qhe,khe->hqk/dot_general | solution.py:976
  318.3 6.4 %multiply_convert_fusion = bf16[4,512,1536]{2,1,0:T(8,128)(2,1)S(1)} fusion(f32[4,512,1536]{2,1,0:T(8,128)} %get-tuple-element.126, f32[4,512,1536]{2,1,0:T(8,128)S(1)} %bitcast.194, f32[4,512]{1,0:T(4,128)S(1)} %get-tuple-element.125, f32[4,512]{1,0:T(4,128)S(1)} %log_add_fusion), kind=kLoop, calls=%fused_computation | loop fusion | flops 12582912 | bytes 31473664 | tf_op jit(solution)/shard_map/convert_element_type | solution.py:978
  350.0 3.7 multiply_reduce_fusion.1
  356.2 39.7 %psum.7 = f32[9216]{0:T(1024)S(1)} all-reduce(f32[9216]{0:T(1024)S(1)} %pad_maximum_fusion.10), channel_id=1, replica_groups=mesh['dp'=8,'mp'=4] {'dp','mp'}, use_global_device_ids=true, to_apply=%region_11.12 | all-reduce | flops 9216 | bytes 73728 | tf_op jit(solution)/shard_map/psum | solution.py:1021
  404.0 9.0 %collective-permute-done.11 = bf16[1024,128]{1,0:T(8,128)(2,1)S(1)} collective-permute-done((bf16[1024,128]{1,0:T(8,128)(2,1)S(1)}, bf16[1024,128]{1,0:T(8,128)(2,1)S(1)}, u32[]{:S(2)}, u32[]{:S(2)}) %collective-permute-start.11) | collective-permute-done | bytes 262176 | tf_op jit(solution)/shard_map/ppermute | solution.py:893
  414.3 10.9 %collective-permute-done.19 = bf16[256,1024]{1,0:T(8,128)(2,1)S(1)} collective-permute-done((bf16[256,1024]{1,0:T(8,128)(2,1)S(1)}, bf16[256,1024]{1,0:T(8,128)(2,1)S(1)}, u32[]{:S(2)}, u32[]{:S(2)}) %collective-permute-start.19) | collective-permute-done | bytes 524320 | tf_op jit(solution)/shard_map/ppermute | solution.py:896
  430.8 90.1 %final_exchange.1 = (bf16[1024,256]{1,0:T(8,128)(2,1)S(1)}, bf16[1024,256]{1,0:T(8,128)(2,1)S(1)}, bf16[1024,256]{1,0:T(8,128)(2,1)S(1)}, bf16[256,1024]{1,0:T(8...) custom-call(bf16[2,1024,256]{2,1,0:T(8,128)(2,1)S(1)} %copy-done.24,, ...), custom_call_target="tpu_custom_call" | custom-call | tf_op jit(solution)/shard_map/final_exchange/pallas_call | solution.py:858
  528.5 5.3 copy.65
  533.9 5.3 copy.66
  539.2 4.2 bitcast_convert_fusion
  (268 shorter events, 124.1 us)
Async XLA Ops:
  0.7 123.0 %copy-start.67 = (s32[2]{0:T(128)S(1)}, s32[2]{0:T(128)}, u32[]{:S(2)}) copy-start(s32[2]{0:T(128)} %param.23) | copy-start | bytes 28
  3.0 203.6 %collective-permute-start.6 = (bf16[128,1024]{1,0:T(8,128)(2,1)}, bf16[128,1024]{1,0:T(8,128)(2,1)}, u32[]{:S(2)}, u32[]{:S(2)}) collective-permute-start(bf16[128,1024]{1,0:T(8,128)(2,1)} %constant_dynamic-slice_fusion.4), channel_id=1, source_target_pairs={{0,3},{1,0},{2,1},{3,2},{4,7},{5,4},{6,5},{7,6},{8,11},{9,8},{10,9... | collective-permute-start | bytes 786440 | tf_op jit(solution)/shard_map/ppermute | solution.py:893
  3.0 204.3 %collective-permute-start.5 = (bf16[128,1024]{1,0:T(8,128)(2,1)}, bf16[128,1024]{1,0:T(8,128)(2,1)}, u32[]{:S(2)}, u32[]{:S(2)}) collective-permute-start(bf16[128,1024]{1,0:T(8,128)(2,1)} %constant_dynamic-slice_fusion.4), channel_id=1, source_target_pairs={{0,2},{1,3},{2,0},{3,1},{4,6},{5,7},{6,4},{7,5},{8,10},{9,11},{10,... | collective-permute-start | bytes 786440 | tf_op jit(solution)/shard_map/ppermute | solution.py:893
  6.4 196.7 %copy-start.59 = (bf16[1024,128]{1,0:T(8,128)(2,1)}, bf16[1024,128]{1,0:T(8,128)(2,1)S(1)}, u32[]{:S(2)}) copy-start(bf16[1024,128]{1,0:T(8,128)(2,1)S(1)} %constant_dynamic-slice_fusion.3) | copy-start | bytes 786436
  6.4 194.5 %collective-permute-start.9 = (bf16[1024,128]{1,0:T(8,128)(2,1)S(1)}, bf16[1024,128]{1,0:T(8,128)(2,1)}, u32[]{:S(2)}, u32[]{:S(2)}) collective-permute-start(bf16[1024,128]{1,0:T(8,128)(2,1)S(1)} %constant_dynamic-slice_fusion.3), channel_id=1, source_target_pairs={{0,3},{1,0},{2,1},{3,2},{4,7},{5,4},{6,5},{7,6},{8,11},{9,8},{10,9... | collective-permute-start | bytes 786440 | tf_op jit(solution)/shard_map/ppermute | solution.py:893
  7.5 193.5 %collective-permute-start.8 = (bf16[1024,128]{1,0:T(8,128)(2,1)S(1)}, bf16[1024,128]{1,0:T(8,128)(2,1)}, u32[]{:S(2)}, u32[]{:S(2)}) collective-permute-start(bf16[1024,128]{1,0:T(8,128)(2,1)S(1)} %constant_dynamic-slice_fusion.3), channel_id=1, source_target_pairs={{0,2},{1,3},{2,0},{3,1},{4,6},{5,7},{6,4},{7,5},{8,10},{9,11},{10,... | collective-permute-start | bytes 786440 | tf_op jit(solution)/shard_map/ppermute | solution.py:893
  9.9 192.9 %collective-permute-start.7 = (bf16[1024,128]{1,0:T(8,128)(2,1)S(1)}, bf16[1024,128]{1,0:T(8,128)(2,1)}, u32[]{:S(2)}, u32[]{:S(2)}) collective-permute-start(bf16[1024,128]{1,0:T(8,128)(2,1)S(1)} %constant_dynamic-slice_fusion.3), channel_id=1, source_target_pairs={{0,1},{1,2},{2,3},{3,0},{4,5},{5,6},{6,7},{7,4},{8,9},{9,10},{10,1... | collective-permute-start | bytes 786440 | tf_op jit(solution)/shard_map/ppermute | solution.py:893
  165.8 34.4 %copy-start.9 = (bf16[2,128,1024]{2,1,0:T(8,128)(2,1)S(1)}, bf16[2,128,1024]{2,1,0:T(8,128)(2,1)}, u32[]{:S(2)}) copy-start(bf16[2,128,1024]{2,1,0:T(8,128)(2,1)} %cot.1) | copy-start | bytes 1572868
  200.9 8.0 %collective-permute-start.4 = (bf16[128,1024]{1,0:T(8,128)(2,1)}, bf16[128,1024]{1,0:T(8,128)(2,1)S(1)}, u32[]{:S(2)}, u32[]{:S(2)}) collective-permute-start(bf16[128,1024]{1,0:T(8,128)(2,1)} %constant_dynamic-slice_fusion.4), channel_id=1, source_target_pairs={{0,1},{1,2},{2,3},{3,0},{4,5},{5,6},{6,7},{7,4},{8,9},{9,10},{10,1... | collective-permute-start | bytes 786440 | tf_op jit(solution)/shard_map/ppermute | solution.py:893
  201.0 20.1 %collective-permute-start.2 = (bf16[256,1024]{1,0:T(8,128)(2,1)}, bf16[256,1024]{1,0:T(8,128)(2,1)S(1)}, u32[]{:S(2)}, u32[]{:S(2)}) collective-permute-start(bf16[256,1024]{1,0:T(8,128)(2,1)} %fusion.142.cot), channel_id=1, source_target_pairs={{0,24},{4,28},{8,0},{12,4},{16,8},{20,12},{24,16},{28,20},{1,25},{... | collective-permute-start | bytes 1572872 | tf_op jit(solution)/shard_map/ppermute | solution.py:896
  202.8 18.2 %collective-permute-start.1 = (bf16[256,1024]{1,0:T(8,128)(2,1)}, bf16[256,1024]{1,0:T(8,128)(2,1)S(1)}, u32[]{:S(2)}, u32[]{:S(2)}) collective-permute-start(bf16[256,1024]{1,0:T(8,128)(2,1)} %fusion.142.cot), channel_id=1, source_target_pairs={{0,16},{4,20},{8,24},{12,28},{16,0},{20,4},{24,8},{28,12},{1,17},{... | collective-permute-start | bytes 1572872 | tf_op jit(solution)/shard_map/ppermute | solution.py:896
  206.6 20.2 %collective-permute-start = (bf16[256,1024]{1,0:T(8,128)(2,1)}, bf16[256,1024]{1,0:T(8,128)(2,1)S(1)}, u32[]{:S(2)}, u32[]{:S(2)}) collective-permute-start(bf16[256,1024]{1,0:T(8,128)(2,1)} %fusion.142.cot), channel_id=1, source_target_pairs={{0,8},{4,12},{8,16},{12,20},{16,24},{20,28},{24,0},{28,4},{1,9},{5... | collective-permute-start | bytes 1572872 | tf_op jit(solution)/shard_map/ppermute | solution.py:896
  216.5 29.6 %collective-permute-start.16 = (bf16[4,256,1024]{2,1,0:T(8,128)(2,1)}, bf16[4,256,1024]{2,1,0:T(8,128)(2,1)}, u32[]{:S(2)}, u32[]{:S(2)}) collective-permute-start(bf16[4,256,1024]{2,1,0:T(8,128)(2,1)} %slice_bitcast_fusion), channel_id=1, source_target_pairs={{0,4},{4,0},{8,12},{12,8},{16,20},{20,16},{24,28},{28,24},{1,5},{5... | collective-permute-start | bytes 6291464 | tf_op jit(solution)/shard_map/ppermute | solution.py:899
  230.9 21.0 %collective-permute-start.3 = (bf16[4,256,1024]{2,1,0:T(8,128)(2,1)}, bf16[4,256,1024]{2,1,0:T(8,128)(2,1)}, u32[]{:S(2)}, u32[]{:S(2)}) collective-permute-start(bf16[4,256,1024]{2,1,0:T(8,128)(2,1)} %get-tuple-element.103), channel_id=1, source_target_pairs={{0,4},{4,0},{8,12},{12,8},{16,20},{20,16},{24,28},{28,24},{1,5},{5... | collective-permute-start | bytes 6291464 | tf_op jit(solution)/shard_map/ppermute | solution.py:899
  270.9 38.6 %slice-start = ((s8[12582912]{0:T(1024)(128)(4,1)}), s8[4194304]{0:T(1024)(128)(4,1)S(1)}, s32[]{:S(2)}) async-start(s8[12582912]{0:T(1024)(128)(4,1)} %bitcast.193), calls=%async_computation | async-start | bytes 8388608
  270.9 38.6 %slice-start.1 = ((s8[12582912]{0:T(1024)(128)(4,1)}), s8[4194304]{0:T(1024)(128)(4,1)S(1)}, s32[]{:S(2)}) async-start(s8[12582912]{0:T(1024)(128)(4,1)} %bitcast.193), calls=%async_computation.1 | async-start | bytes 8388608
  274.8 33.0 %copy-start.53 = (bf16[4,128,512]{2,1,0:T(8,128)(2,1)S(1)}, bf16[4,128,512]{2,1,0:T(8,128)(2,1)}, u32[]{:S(2)}) copy-start(bf16[4,128,512]{2,1,0:T(8,128)(2,1)} %copy-done.52) | copy-start | bytes 1572868
  274.8 34.7 %slice-start.2 = ((s8[12582912]{0:T(1024)(128)(4,1)}), s8[4194304]{0:T(1024)(128)(4,1)S(1)}, s32[]{:S(2)}) async-start(s8[12582912]{0:T(1024)(128)(4,1)} %bitcast.193), calls=%async_computation.2 | async-start | bytes 8388608
  330.0 66.5 %collective-permute-start.13 = (bf16[128,1024]{1,0:T(8,128)(2,1)}, bf16[128,1024]{1,0:T(8,128)(2,1)}, u32[]{:S(2)}, u32[]{:S(2)}) collective-permute-start(bf16[128,1024]{1,0:T(8,128)(2,1)} %get-tuple-element.104), channel_id=1, source_target_pairs={{0,3},{1,0},{2,1},{3,2},{4,7},{5,4},{6,5},{7,6},{8,11},{9,8},{10,9... | collective-permute-start | bytes 786440 | tf_op jit(solution)/shard_map/ppermute | solution.py:893
  331.4 67.1 %collective-permute-start.15 = (bf16[128,1024]{1,0:T(8,128)(2,1)}, bf16[128,1024]{1,0:T(8,128)(2,1)}, u32[]{:S(2)}, u32[]{:S(2)}) collective-permute-start(bf16[128,1024]{1,0:T(8,128)(2,1)} %get-tuple-element.105), channel_id=1, source_target_pairs={{0,1},{1,2},{2,3},{3,0},{4,5},{5,6},{6,7},{7,4},{8,9},{9,10},{10,1... | collective-permute-start | bytes 786440 | tf_op jit(solution)/shard_map/ppermute | solution.py:893
  331.5 69.3 %collective-permute-start.14 = (bf16[128,1024]{1,0:T(8,128)(2,1)}, bf16[128,1024]{1,0:T(8,128)(2,1)}, u32[]{:S(2)}, u32[]{:S(2)}) collective-permute-start(bf16[128,1024]{1,0:T(8,128)(2,1)} %get-tuple-element.106), channel_id=1, source_target_pairs={{0,2},{1,3},{2,0},{3,1},{4,6},{5,7},{6,4},{7,5},{8,10},{9,11},{10,... | collective-permute-start | bytes 786440 | tf_op jit(solution)/shard_map/ppermute | solution.py:893
  333.6 67.3 %collective-permute-start.10 = (bf16[1024,128]{1,0:T(8,128)(2,1)}, bf16[1024,128]{1,0:T(8,128)(2,1)}, u32[]{:S(2)}, u32[]{:S(2)}) collective-permute-start(bf16[1024,128]{1,0:T(8,128)(2,1)} %get-tuple-element.107), channel_id=1, source_target_pairs={{0,3},{1,0},{2,1},{3,2},{4,7},{5,4},{6,5},{7,6},{8,11},{9,8},{10,9... | collective-permute-start | bytes 786440 | tf_op jit(solution)/shard_map/ppermute | solution.py:893
  333.6 68.6 %collective-permute-start.12 = (bf16[1024,128]{1,0:T(8,128)(2,1)}, bf16[1024,128]{1,0:T(8,128)(2,1)}, u32[]{:S(2)}, u32[]{:S(2)}) collective-permute-start(bf16[1024,128]{1,0:T(8,128)(2,1)} %get-tuple-element.108), channel_id=1, source_target_pairs={{0,1},{1,2},{2,3},{3,0},{4,5},{5,6},{6,7},{7,4},{8,9},{9,10},{10,1... | collective-permute-start | bytes 786440 | tf_op jit(solution)/shard_map/ppermute | solution.py:893
  350.0 50.8 %copy-start.58 = (bf16[256,1024]{1,0:T(8,128)(2,1)S(1)}, bf16[256,1024]{1,0:T(8,128)(2,1)}, u32[]{:S(2)}) copy-start(bf16[256,1024]{1,0:T(8,128)(2,1)} %get-tuple-element.100) | copy-start | bytes 1572868
  350.0 50.9 %copy-start.57 = (bf16[256,1024]{1,0:T(8,128)(2,1)S(1)}, bf16[256,1024]{1,0:T(8,128)(2,1)}, u32[]{:S(2)}) copy-start(bf16[256,1024]{1,0:T(8,128)(2,1)} %get-tuple-element.101) | copy-start | bytes 1572868
  354.6 70.7 %copy-start.65 = (f32[1024]{0:T(1024)S(1)}, f32[1024]{0:T(1024)}, u32[]{:S(2)}) copy-start(f32[1024]{0:T(1024)} %param.35) | copy-start | bytes 12292
  356.1 71.0 %copy-start.62 = (f32[1024]{0:T(1024)S(1)}, f32[1024]{0:T(1024)}, u32[]{:S(2)}) copy-start(f32[1024]{0:T(1024)} %param.24) | copy-start | bytes 12292
  396.5 30.6 %collective-permute-start.20 = (f32[256,1024]{1,0:T(8,128)S(1)}, f32[256,1024]{1,0:T(8,128)S(1)}, u32[]{:S(2)}, u32[]{:S(2)}) collective-permute-start(f32[256,1024]{1,0:T(8,128)S(1)} %constant_dynamic-slice_fusion.1), channel_id=1, source_target_pairs={{0,4},{4,0},{8,12},{12,8},{16,20},{20,16},{24,28},{28,24},{1,5},{5... | collective-permute-start | bytes 3145736 | tf_op jit(solution)/shard_map/ppermute | solution.py:899
  398.5 15.8 %collective-permute-start.17 = (bf16[256,1024]{1,0:T(8,128)(2,1)}, bf16[256,1024]{1,0:T(8,128)(2,1)S(1)}, u32[]{:S(2)}, u32[]{:S(2)}) collective-permute-start(bf16[256,1024]{1,0:T(8,128)(2,1)} %get-tuple-element.99), channel_id=1, source_target_pairs={{0,24},{4,28},{8,0},{12,4},{16,8},{20,12},{24,16},{28,20},{1,25},{... | collective-permute-start | bytes 1572872 | tf_op jit(solution)/shard_map/ppermute | solution.py:896
  400.7 24.5 %collective-permute-start.19 = (bf16[256,1024]{1,0:T(8,128)(2,1)S(1)}, bf16[256,1024]{1,0:T(8,128)(2,1)S(1)}, u32[]{:S(2)}, u32[]{:S(2)}) collective-permute-start(bf16[256,1024]{1,0:T(8,128)(2,1)S(1)} %copy-done.58), channel_id=1, source_target_pairs={{0,8},{4,12},{8,16},{12,20},{16,24},{20,28},{24,0},{28,4},{1,9},{5... | collective-permute-start | bytes 1572872 | tf_op jit(solution)/shard_map/ppermute | solution.py:896
  400.9 24.4 %collective-permute-start.18 = (bf16[256,1024]{1,0:T(8,128)(2,1)S(1)}, bf16[256,1024]{1,0:T(8,128)(2,1)S(1)}, u32[]{:S(2)}, u32[]{:S(2)}) collective-permute-start(bf16[256,1024]{1,0:T(8,128)(2,1)S(1)} %copy-done.57), channel_id=1, source_target_pairs={{0,16},{4,20},{8,24},{12,28},{16,0},{20,4},{24,8},{28,12},{1,17},{... | collective-permute-start | bytes 1572872 | tf_op jit(solution)/shard_map/ppermute | solution.py:896
  402.2 10.8 %collective-permute-start.11 = (bf16[1024,128]{1,0:T(8,128)(2,1)S(1)}, bf16[1024,128]{1,0:T(8,128)(2,1)S(1)}, u32[]{:S(2)}, u32[]{:S(2)}) collective-permute-start(bf16[1024,128]{1,0:T(8,128)(2,1)S(1)} %get-tuple-element.109), channel_id=1, source_target_pairs={{0,2},{1,3},{2,0},{3,1},{4,6},{5,7},{6,4},{7,5},{8,10},{9,11},{10,... | collective-permute-start | bytes 786440 | tf_op jit(solution)/shard_map/ppermute | solution.py:893
  (64 other events, 314.7 us)
